TPU v7x, 32 devices: a whole 2x2x4 slice. The times are simulated.
32 devices in a mesh: blk: 8 (over y, x, core), space: 4 (over z).
Axes of the slice: x: 2, y: 2, z: 4, core: 2. Of those that a mesh axis runs over, the one named last changes fastest.
Arguments:
- electrons: bfloat16 [8, 8, 2, 64, 4096], P('blk', None, None, 'space'), may hold values from -4 to 4
- holes: bfloat16 [8, 8, 2, 64, 4096], P('blk', None, None, 'space'), may hold values from -4 to 4
- pair_order: int32 [8, 2], P('blk'), may hold values from 0 to 1, each once within a row
Outputs:
- potential: float32 [8, 2, 64, 64, 128], P('blk', None, 'space')
- coulomb: float32 [8, 2, 2, 2], P('blk')
Inputs may be any that keep to these rules, and one draw needn't show every extreme that they name: `pair_order`: each row lists every candidate once.
All inputs are finite; a program needn't handle non-finite values.
Results may differ from a plain program's by a relative error of at most 0.0003.
Values may be sent and summed in bfloat16 or wider, within the bound.
A program may use at most 64 MiB of HBM per device.

v0:
```python
from functools import partial
import math
import jax
import jax.numpy as jnp
from jax import lax
from jax.sharding import PartitionSpec as P

NX = 64
NY = 64
NZ = 64
SCREENING = 0.01
PRECISE = lax.Precision.HIGHEST


def shifted(block, axis, distance):
    devices = range(lax.axis_size(axis))
    route = [((i - distance) % len(devices), i) for i in devices]
    return lax.ppermute(block, axis, route)


def phase_tables(points, direction):
    positions = jnp.arange(points, dtype=jnp.int32)
    products = positions[:, None] * positions[None, :] % points
    angles = 2.0 * math.pi / points * products.astype(jnp.float32)
    return (jnp.cos(angles), direction * jnp.sin(angles))


def depth_matrix(points, direction):
    cosines, sines = phase_tables(points, direction)
    upper = jnp.concatenate([cosines, -sines], axis=1)
    lower = jnp.concatenate([sines, cosines], axis=1)
    return jnp.concatenate([upper, lower], axis=0)


def turned(values):
    middle = values.shape[-1] // 2
    return jnp.concatenate([values[..., middle:], -values[..., :middle]], axis=-1)


def along_rows(values, direction):
    cosines, sines = phase_tables(values.shape[1], direction)
    tables = jnp.stack([cosines, sines])
    stacked = jnp.stack([values, turned(values)])
    return jnp.einsum("tkn,tpnbc->pkbc", tables, stacked, precision=PRECISE)


def along_columns(values, direction):
    cosines, sines = phase_tables(values.shape[2], direction)
    tables = jnp.stack([cosines, sines])
    stacked = jnp.stack([values, turned(values)])
    return jnp.einsum("tkn,tpanc->pakc", tables, stacked, precision=PRECISE)


def along_depth(values, direction):
    matrix = depth_matrix(values.shape[-1] // 2, direction)
    return jnp.einsum("pabn,nk->pabk", values, matrix, precision=PRECISE)


def lattice_term(indices, points):
    return 2.0 - 2.0 * jnp.cos(2.0 * math.pi / points * (indices % points).astype(jnp.float32))


def green_block(start_y, rows_y):
    index_x = jnp.arange(NX, dtype=jnp.int32)
    index_y = start_y + jnp.arange(rows_y, dtype=jnp.int32)
    index_z = jnp.arange(2 * NZ, dtype=jnp.int32)
    term_x = lattice_term(index_x, NX)
    term_y = lattice_term(index_y, NY)
    term_z = lattice_term(index_z, NZ)
    green = 1.0 / (
        term_x[:, None, None] + term_y[None, :, None] + term_z[None, None, :] + SCREENING
    )
    anchor = (
        (index_x[:, None, None] == 0)
        & (index_y[None, :, None] == 0)
        & (index_z[None, None, :] % NZ == 0)
    )
    return jnp.where(anchor, jnp.zeros_like(green), green)


def pair_densities(electrons, hole_set):

    def banded(first_set, second_set):
        return jnp.einsum(
            "ebxc,hbxc->hexc", first_set, second_set, preferred_element_type=jnp.float32
        )

    real_part = banded(electrons[:, :, 0], hole_set[:, :, 0]) + banded(
        electrons[:, :, 1], hole_set[:, :, 1]
    )
    imag_part = banded(electrons[:, :, 0], hole_set[:, :, 1]) - banded(
        electrons[:, :, 1], hole_set[:, :, 0]
    )
    target_shape = (real_part.shape[0] * real_part.shape[1], real_part.shape[2], NY, NZ)
    return jnp.concatenate(
        [real_part.reshape(target_shape), imag_part.reshape(target_shape)], axis=-1
    )


def fetch_previous(holes):
    return shifted(holes, "blk", 1)


def plane_spectra(densities):
    return along_columns(along_depth(densities, 1.0), 1.0)


def column_spectra(block, start_y):
    spectra = along_rows(block, 1.0)
    return (spectra, spectra * green_block(start_y, block.shape[2])[None])


def finish_inverse(block, factor):
    return along_depth(along_columns(block, -1.0), -1.0) * factor


def inverse_field(weighted, factor):
    return finish_inverse(
        lax.all_to_all(
            along_rows(weighted, -1.0), "space", split_axis=1, concat_axis=2, tiled=True
        ),
        factor=factor,
    )


def pair_products(first_set, second_set):
    flat_first = first_set.reshape(first_set.shape[0], -1)
    stacked = jnp.stack([second_set, -turned(second_set)]).reshape(2, second_set.shape[0], -1)
    return jnp.einsum("pn,tqn->tpq", flat_first, stacked, precision=PRECISE)


def shards(electrons, holes, pair_order):
    rows_y = NY // lax.axis_size("space")
    start_y = lax.axis_index("space") * rows_y
    factor = 1.0 / (NX * NY * NZ)
    forward = partial(column_spectra, start_y=start_y)
    previous = fetch_previous(holes)
    densities = pair_densities(electrons, jnp.concatenate([holes, previous], axis=0))
    spectra, weighted = forward(
        lax.all_to_all(plane_spectra(densities), "space", split_axis=2, concat_axis=1, tiled=True)
    )
    partial_sums = pair_products(weighted, spectra) * (factor * factor)
    potential_field = inverse_field(weighted, factor)
    totals = lax.psum(partial_sums, "space")
    pair_rank = pair_order[0]
    coulomb = jnp.take(jnp.take(totals, pair_rank, axis=1), pair_rank, axis=2)
    potential = jnp.take(potential_field, pair_rank, axis=0)
    return (potential[None], coulomb[None])


def solution(mesh):
    in_specs = (
        P("blk", None, None, "space", None),
        P("blk", None, None, "space", None),
        P("blk", None),
    )
    out_specs = (P("blk", None, "space", None, None), P("blk", None, None, None))
    return jax.shard_map(shards, mesh=mesh, in_specs=in_specs, out_specs=out_specs, check_vma=False)
```

profile of v0, /device:TPU:0, one launch (start us, length us, event | category | flops | bytes accessed | tf_op | source)
XLA Modules:
  0.0 122.4 jit_solution(10038824163050638869)
XLA Ops:
  0.6 0.5 collective-permute-start
  1.7 1.9 %constant_dynamic-update-slice_fusion.1 = bf16[2,8,2,16,4096]{4,3,2,1,0:T(8,128)(2,1)S(1)} fusion(bf16[1,8,2,16,4096]{4,3,2,1,0:T(8,128)(2,1)} %param.4), kind=kLoop, calls=%fused_computation.107 | loop fusion | bytes 4194304
  4.4 23.6 %collective-permute-done = bf16[1,8,2,16,4096]{4,3,2,1,0:T(8,128)(2,1)S(1)} collective-permute-done((bf16[1,8,2,16,4096]{4,3,2,1,0:T(8,128)(2,1)}, bf16[1,8,2,16,4096]{4,3,2,1,0:T(8,128)(2,1)S(1)}, u32[]{:S(2)}, u32[]{:S(2)}) %collective-permute-start) | collective-permute-done | bytes 2097184 | tf_op jit(solution)/shard_map/ppermute | solution.py:18
  28.2 1.7 %fusion.2 = (f32[16,4096,2]{1,0,2:T(8,128)S(1)}, f32[16,4096,2]{1,0,2:T(8,128)S(1)}, f32[16,4096,2]{1,0,2:T(8,128)S(1)}, f32[16,4096,2]{1,0,2:T(8,128)S(1)}) fusion(f32[16,4096,8]{1,0,2:T(8,128)S(1)} %get-tuple-element.9, bf16[2,8,2,16,4096]{4,3,2,1,0:T(8,128)(2,1)S(1)} %constant_dynamic-update-slice_fusion, f32[16,4096,8]{1,0,2:T(8,128)S(1)} %get-tuple-element.8), kind=kLoop, calls=%fused_computation.9 | loop fusion | flops 9961472 | bytes 10485760 | tf_op jit(solution)/shard_map/ebxc,hbxc->hexc/dot_general | solution.py:84
  30.8 1.1 fusion.32
  32.7 1.3 %fusion.16 = f32[2,16,64,128]{3,2,0,1:T(8,128)S(1)} fusion(f32[1,64,64]{2,1,0:T(8,128)S(1)} %get-tuple-element.27, f32[1,64,64]{2,1,0:T(8,128)S(1)} %get-tuple-element.26, f32[1,2,16,64,128]{4,3,2,1,0:T(8,128)S(1)} %maximum_bitcast_fusion, f32[1,2,16,64,128]{4,3,2,1,0:T(8,128)S(1)} %bitcast.148), kind=kOutput, calls=%fused_computation.29 | convolution fusion | flops 403185664 | bytes 3178496 | tf_op jit(solution)/shard_map/tkn,tpanc->pakc/dot_general | solution.py:51
  34.0 1.6 %copy.36 = f32[2,16,64,128]{3,1,0,2:T(8,128)} copy(f32[2,16,64,128]{3,2,0,1:T(8,128)S(1)} %fusion.16) | data formatting | bytes 2097152 | tf_op jit(solution)/shard_map/tkn,tpanc->pakc/transpose | solution.py:51
  35.6 5.6 %all-to-all-start = ((f32[2,16,64,128]{3,1,0,2:T(8,128)}), f32[2,16,64,128]{3,1,0,2:T(8,128)S(1)}, u32[]{:S(2)}, u32[]{:S(2)}) async-start(f32[2,16,64,128]{3,1,0,2:T(8,128)} %copy.36), calls=%async_computation | async-start | bytes 2097152 | tf_op jit(solution)/shard_map/all_to_all | solution.py:140
  41.6 1.1 divide_select_fusion
  42.8 22.7 %all-to-all-done = f32[2,16,64,128]{3,1,0,2:T(8,128)S(1)} async-done(((f32[2,16,64,128]{3,1,0,2:T(8,128)}), f32[2,16,64,128]{3,1,0,2:T(8,128)S(1)}, u32[]{:S(2)}, u32[]{:S(2)}) %all-to-all-start) | async-done | bytes 1048608 | tf_op jit(solution)/shard_map/all_to_all | solution.py:140
  66.3 0.7 copy-done.1
  67.0 1.3 %broadcast_multiply_fusion = (f32[2,64,16,128]{3,1,2,0:T(8,128)S(1)}, f32[2,16,128,64,1]{2,3,4,1,0:T(8,128)S(1)}) fusion(f32[64,16,128]{2,0,1:T(8,128)S(1)} %copy-done.1, f32[1,64,64]{2,1,0:T(8,128)S(1)} %get-tuple-element.26, f32[1,64,64]{2,1,0:T(8,128)S(1)} %get-tuple-element.27, f32[1,2,64,16,128]{4,2,0,3,1:T(8,128)S(1)} %maximum_bitcast_fusion.1, ...), kind=kOutput, calls=%fused_computation.58 | convolution fusion | flops 403447808 | bytes 4751360 | tf_op jit(solution)/shard_map/tkn,tpnbc->pkbc/dot_general | solution.py:44
  69.1 1.3 %fusion.19 = f32[2,64,16,128]{3,1,0,2:T(8,128)S(1)} fusion(f32[1,64,64]{2,1,0:T(8,128)S(1)} %get-tuple-element.27, f32[1,64,64]{2,1,0:T(8,128)S(1)} %broadcast_multiply_fusion.2, f32[1,2,64,16,128]{4,2,3,1,0:T(8,128)S(1)} %maximum_bitcast_fusion.2, f32[1,2,64,16,128]{4,2,3,1,0:T(8,128)S(1)} %bitcast.151), kind=kOutput, calls=%fused_computation.30 | convolution fusion | flops 403185664 | bytes 3178496 | tf_op jit(solution)/shard_map/tkn,tpnbc->pkbc/dot_general | solution.py:44
  70.4 1.6 %copy.38 = f32[2,64,16,128]{3,2,0,1:T(8,128)} copy(f32[2,64,16,128]{3,1,0,2:T(8,128)S(1)} %fusion.19) | data formatting | bytes 2097152 | tf_op jit(solution)/shard_map/tkn,tpnbc->pkbc/transpose | solution.py:44
  72.0 3.5 %all-to-all-start.1 = ((f32[2,64,16,128]{3,2,0,1:T(8,128)}), f32[2,64,16,128]{3,2,0,1:T(8,128)S(1)}, u32[]{:S(2)}, u32[]{:S(2)}) async-start(f32[2,64,16,128]{3,2,0,1:T(8,128)} %copy.38), calls=%async_computation.1 | async-start | bytes 2097152 | tf_op jit(solution)/shard_map/all_to_all | solution.py:119
  76.7 26.4 %fusion.28 = f32[2,2,2]{1,2,0:T(2,128)S(1)} fusion(f32[2,2,64,16,128]{4,2,3,1,0:T(8,128)S(1)} %pad_maximum_fusion.3, f32[2,64,16,128]{3,1,2,0:T(8,128)S(1)} %get-tuple-element.20), kind=kOutput, calls=%fused_computation.34 | convolution fusion | flops 12582920 | bytes 3145760 | tf_op jit(solution)/shard_map/pn,tqn->tpq/dot_general | solution.py:129
  103.1 12.2 %psum.7 = f32[2,2,2]{1,2,0:T(2,128)S(1)} all-reduce(f32[2,2,2]{1,2,0:T(2,128)S(1)} %fusion.28), channel_id=1, replica_groups=mesh['blk'=8,'space'=4] {'space'}, use_global_device_ids=true, to_apply=%region_0.1 | all-reduce | flops 8 | bytes 64 | tf_op jit(solution)/shard_map/psum | solution.py:144
  115.3 0.6 gather_fusion.1
  116.1 0.6 gather_fusion.2
  116.8 0.6 bitcast_select_fusion.1
  118.2 1.3 %fusion.8 = f32[2,16,128,64,1]{2,3,0,1,4:T(8,128)S(1)} fusion(f32[1,64,64]{2,1,0:T(8,128)S(1)} %get-tuple-element.27, f32[1,64,64]{2,1,0:T(8,128)S(1)} %broadcast_multiply_fusion.2, f32[1,2,16,64,128]{4,3,2,1,0:T(8,128)S(1)} %maximum_bitcast_fusion.3, f32[1,2,16,64,128]{4,3,2,1,0:T(8,128)S(1)} %bitcast.150), kind=kOutput, calls=%fused_computation.21 | convolution fusion | flops 403185664 | bytes 3178496 | tf_op jit(solution)/shard_map/tkn,tpanc->pakc/dot_general | solution.py:51
  119.5 1.0 convolution_multiply_fusion
  120.6 0.6 gather_fusion
  121.2 1.2 bitcast_select_fusion
  (44 shorter events, 7.6 us)
Async XLA Ops:
  0.6 27.3 %collective-permute-start = (bf16[1,8,2,16,4096]{4,3,2,1,0:T(8,128)(2,1)}, bf16[1,8,2,16,4096]{4,3,2,1,0:T(8,128)(2,1)S(1)}, u32[]{:S(2)}, u32[]{:S(2)}) collective-permute-start(bf16[1,8,2,16,4096]{4,3,2,1,0:T(8,128)(2,1)} %param.4), channel_id=1, source_target_pairs={{28,0},{0,4},{4,8},{8,12},{12,16},{16,20},{20,24},{24,28},{29,1},{... | collective-permute-start | bytes 6291464 | tf_op jit(solution)/shard_map/ppermute | solution.py:18
  1.7 2.2 %copy-start = (bf16[1,8,2,16,4096]{4,3,2,1,0:T(8,128)(2,1)S(1)}, bf16[1,8,2,16,4096]{4,3,2,1,0:T(8,128)(2,1)}, u32[]{:S(2)}) copy-start(bf16[1,8,2,16,4096]{4,3,2,1,0:T(8,128)(2,1)} %param.3) | copy-start | bytes 6291460
  34.0 7.5 %copy-start.2 = (s32[1,2]{1,0:T(1,128)S(1)}, s32[1,2]{1,0:T(1,128)}, u32[]{:S(2)}) copy-start(s32[1,2]{1,0:T(1,128)} %param.5) | copy-start | bytes 28
  35.6 29.8 %all-to-all-start = ((f32[2,16,64,128]{3,1,0,2:T(8,128)}), f32[2,16,64,128]{3,1,0,2:T(8,128)S(1)}, u32[]{:S(2)}, u32[]{:S(2)}) async-start(f32[2,16,64,128]{3,1,0,2:T(8,128)} %copy.36), calls=%async_computation | async-start | bytes 2097152 | tf_op jit(solution)/shard_map/all_to_all | solution.py:140
  66.0 1.0 copy-start.1
  72.0 45.3 %all-to-all-start.1 = ((f32[2,64,16,128]{3,2,0,1:T(8,128)}), f32[2,64,16,128]{3,2,0,1:T(8,128)S(1)}, u32[]{:S(2)}, u32[]{:S(2)}) async-start(f32[2,64,16,128]{3,2,0,1:T(8,128)} %copy.38), calls=%async_computation.1 | async-start | bytes 2097152 | tf_op jit(solution)/shard_map/all_to_all | solution.py:119
where the time goes:
time: 123 us; the launch traced here: 122 us
  waiting for transfers between devices  46.2 us (38%)
  matrix products  33.8 us (27%)
  blocking collectives  12.2 us (10%)
  other arithmetic  10.2 us (8%)
  starting transfers between devices  9.69 us (8%)
  local copies, waits for them, and re-layouts  9.38 us (8%)
    dot_general x1, matrix products, pair_products(): return jnp.einsum('pn,tqn->tpq', flat_first, stacked, precision=PRECISE)  26.4 us
    ppermute x1, waiting for transfers between devices, shifted(): return lax.ppermute(block, axis, route)  23.6 us
    all_to_all x1, waiting for transfers between devices, shards(): lax.all_to_all(plane_spectra(densities), 'space', split_axis=2, concat_ax...  22.7 us
    psum x1, blocking collectives, shards(): totals = lax.psum(partial_sums, 'space')  12.2 us
    all_to_all x1, starting transfers between devices, shards(): lax.all_to_all(plane_spectra(densities), 'space', split_axis=2, concat_ax...  5.62 us
    all_to_all x1, starting transfers between devices, inverse_field(): lax.all_to_all(along_rows(weighted, -1.0), 'space', split_axis=1, concat_...  3.52 us
    unnamed x7, local copies, waits for them, and re-layouts  2.91 us
    dot_general x2, matrix products, along_rows(): return jnp.einsum('tkn,tpnbc->pkbc', tables, stacked, precision=PRECISE)  2.64 us
  transfers between devices with their start and end apart: 3, of which 2 were waited for; matrix products, arithmetic and copies ran while one was open for 28% of the time, Pallas kernels for 0%

commit v1 on v0

--- a/solution.py
+++ b/solution.py
@@ -10,6 +10,22 @@
 NZ = 64
 SCREENING = 0.01
 PRECISE = lax.Precision.HIGHEST
+
+
+def swapped_with_each(x, axis, split, join):
+    ways, here = (lax.axis_size(axis), lax.axis_index(axis))
+    width = x.shape[split] // ways
+    shape = list(x.shape)
+    shape[split] = width
+    height = shape[join]
+    shape[join] = height * ways
+    full = jnp.zeros(shape, x.dtype)
+    for mask in range(ways):
+        part = lax.dynamic_slice_in_dim(x, (here ^ mask) * width, width, axis=split)
+        if mask:
+            part = lax.ppermute(part, axis, [(d, d ^ mask) for d in range(ways)])
+        full = lax.dynamic_update_slice_in_dim(full, part, (here ^ mask) * height, axis=join)
+    return full
 
 
 def shifted(block, axis, distance):
@@ -136,9 +152,7 @@
     forward = partial(column_spectra, start_y=start_y)
     previous = fetch_previous(holes)
     densities = pair_densities(electrons, jnp.concatenate([holes, previous], axis=0))
-    spectra, weighted = forward(
-        lax.all_to_all(plane_spectra(densities), "space", split_axis=2, concat_axis=1, tiled=True)
-    )
+    spectra, weighted = forward(swapped_with_each(plane_spectra(densities), "space", 2, 1))
     partial_sums = pair_products(weighted, spectra) * (factor * factor)
     potential_field = inverse_field(weighted, factor)
     totals = lax.psum(partial_sums, "space")

time: 123 us -> 119 us (0.967)
  waiting for transfers between devices: 46.2 us -> 41.8 us
  other arithmetic: 10.2 us -> 11.5 us
    all_to_all x1 -> x0, waiting for transfers between devices: 22.7 us -> none  [shards(): lax.all_to_all(plane_spectra(densities), 'space', split_axis=2, concat_ax...]
    ppermute x0 -> x3, waiting for transfers between devices: none -> 21 us  [swapped_with_each(): part = lax.ppermute(part, axis, [(d, d ^ mask) for d in range(ways)])]
    all_to_all x1 -> x0, starting transfers between devices: 5.62 us -> none  [shards(): lax.all_to_all(plane_spectra(densities), 'space', split_axis=2, concat_ax...]
    ppermute x0 -> x3, starting transfers between devices: none -> 5.13 us  [swapped_with_each(): part = lax.ppermute(part, axis, [(d, d ^ mask) for d in range(ways)])]
    ppermute x1, waiting for transfers between devices: 23.6 us -> 20.8 us  [shifted(): return lax.ppermute(block, axis, route)]
    transpose x1 -> x0, local copies, waits for them, and re-layouts: 1.58 us -> none  [along_columns(): return jnp.einsum('tkn,tpanc->pakc', tables, stacked, precision=PRECISE)]
    unnamed x7 -> x5, local copies, waits for them, and re-layouts: 2.91 us -> 2.91 us
  transfers between devices with their start and end apart: 3 -> 5, of which waited for: 2 -> 3; matrix products, arithmetic and copies ran while one was open for 28% -> 30% of each run, Pallas kernels for 0% -> 0%
where the time goes in v1:
time: 119 us; the launch traced here: 118 us
  waiting for transfers between devices  41.8 us (35%)
  matrix products  33.8 us (28%)
  blocking collectives  12.2 us (10%)
  other arithmetic  11.5 us (10%)
  starting transfers between devices  9.59 us (8%)
  local copies, waits for them, and re-layouts  8.39 us (7%)
    dot_general x1, matrix products, pair_products(): return jnp.einsum('pn,tqn->tpq', flat_first, stacked, precision=PRECISE)  26.4 us
    ppermute x3, waiting for transfers between devices, swapped_with_each(): part = lax.ppermute(part, axis, [(d, d ^ mask) for d in range(ways)])  21 us
    ppermute x1, waiting for transfers between devices, shifted(): return lax.ppermute(block, axis, route)  20.8 us
    psum x1, blocking collectives, shards(): totals = lax.psum(partial_sums, 'space')  12.2 us
    ppermute x3, starting transfers between devices, swapped_with_each(): part = lax.ppermute(part, axis, [(d, d ^ mask) for d in range(ways)])  5.13 us
    all_to_all x1, starting transfers between devices, inverse_field(): lax.all_to_all(along_rows(weighted, -1.0), 'space', split_axis=1, concat_...  3.92 us
    unnamed x5, local copies, waits for them, and re-layouts  2.91 us
    dot_general x2, matrix products, along_rows(): return jnp.einsum('tkn,tpnbc->pkbc', tables, stacked, precision=PRECISE)  2.64 us
  transfers between devices with their start and end apart: 5, of which 3 were waited for; matrix products, arithmetic and copies ran while one was open for 30% of the time, Pallas kernels for 0%

profile of v1, /device:TPU:0, one launch (start us, length us, event | category | flops | bytes accessed | tf_op | source)
XLA Modules:
  0.0 118.2 jit_solution(894829154672568665)
XLA Ops:
  1.2 0.7 compare_and_fusion
  1.8 0.7 fusion.81
  3.3 1.1 divide_select_fusion
  4.4 1.9 %constant_dynamic-update-slice_fusion.1 = bf16[2,8,2,16,4096]{4,3,2,1,0:T(8,128)(2,1)S(1)} fusion(bf16[1,8,2,16,4096]{4,3,2,1,0:T(8,128)(2,1)} %param.4), kind=kLoop, calls=%fused_computation.115 | loop fusion | bytes 4194304
  7.1 20.8 %collective-permute-done = bf16[1,8,2,16,4096]{4,3,2,1,0:T(8,128)(2,1)S(1)} collective-permute-done((bf16[1,8,2,16,4096]{4,3,2,1,0:T(8,128)(2,1)}, bf16[1,8,2,16,4096]{4,3,2,1,0:T(8,128)(2,1)S(1)}, u32[]{:S(2)}, u32[]{:S(2)}) %collective-permute-start) | collective-permute-done | bytes 2097184 | tf_op jit(solution)/shard_map/ppermute | solution.py:34
  28.2 1.7 %fusion.2 = (f32[16,4096,2]{1,0,2:T(8,128)S(1)}, f32[16,4096,2]{1,0,2:T(8,128)S(1)}, f32[16,4096,2]{1,0,2:T(8,128)S(1)}, f32[16,4096,2]{1,0,2:T(8,128)S(1)}) fusion(f32[16,4096,8]{1,0,2:T(8,128)S(1)} %get-tuple-element.9, bf16[2,8,2,16,4096]{4,3,2,1,0:T(8,128)(2,1)S(1)} %constant_dynamic-update-slice_fusion, f32[16,4096,8]{1,0,2:T(8,128)S(1)} %get-tuple-element.8), kind=kLoop, calls=%fused_computation.9 | loop fusion | flops 9961472 | bytes 10485760 | tf_op jit(solution)/shard_map/ebxc,hbxc->hexc/dot_general | solution.py:100
  30.8 1.1 fusion.29
  32.7 1.3 %fusion.12 = f32[2,16,128,64,1]{2,3,0,1,4:T(8,128)S(1)} fusion(f32[1,64,64]{2,1,0:T(8,128)S(1)} %get-tuple-element.31, f32[1,64,64]{2,1,0:T(8,128)S(1)} %get-tuple-element.30, f32[1,2,16,64,128]{4,3,2,1,0:T(8,128)S(1)} %maximum_bitcast_fusion, f32[1,2,16,64,128]{4,3,2,1,0:T(8,128)S(1)} %bitcast.152), kind=kOutput, calls=%fused_computation.25 | convolution fusion | flops 403185664 | bytes 3178496 | tf_op jit(solution)/shard_map/tkn,tpanc->pakc/dot_general | solution.py:67
  34.2 2.4 %collective-permute-start.1 = (f32[2,16,16,128]{3,2,1,0:T(8,128)S(1)}, f32[2,16,16,128]{3,2,1,0:T(8,128)S(1)}, u32[]{:S(2)}, u32[]{:S(2)}) collective-permute-start(f32[2,16,16,128]{3,2,1,0:T(8,128)S(1)} %get-tuple-element.20), channel_id=1, source_target_pairs={{0,1},{1,0},{2,3},{3,2},{4,5},{5,4},{6,7},{7,6},{8,9},{9,8},{10,11... | collective-permute-start | bytes 786440 | tf_op jit(solution)/shard_map/ppermute | solution.py:26
  36.7 2.5 %collective-permute-start.3 = (f32[2,16,16,128]{3,2,1,0:T(8,128)S(1)}, f32[2,16,16,128]{3,2,1,0:T(8,128)S(1)}, u32[]{:S(2)}, u32[]{:S(2)}) collective-permute-start(f32[2,16,16,128]{3,2,1,0:T(8,128)S(1)} %get-tuple-element.18), channel_id=1, source_target_pairs={{0,3},{1,2},{2,1},{3,0},{4,7},{5,6},{6,5},{7,4},{8,11},{9,10},{10,... | collective-permute-start | bytes 786440 | tf_op jit(solution)/shard_map/ppermute | solution.py:26
  39.7 3.6 %collective-permute-done.1 = f32[2,16,16,128]{3,2,1,0:T(8,128)S(1)} collective-permute-done((f32[2,16,16,128]{3,2,1,0:T(8,128)S(1)}, f32[2,16,16,128]{3,2,1,0:T(8,128)S(1)}, u32[]{:S(2)}, u32[]{:S(2)}) %collective-permute-start.1) | collective-permute-done | bytes 262176 | tf_op jit(solution)/shard_map/ppermute | solution.py:26
  43.4 17.4 %collective-permute-done.2 = f32[2,16,16,128]{3,2,1,0:T(8,128)S(1)} collective-permute-done((f32[2,16,16,128]{3,2,1,0:T(8,128)S(1)}, f32[2,16,16,128]{3,2,1,0:T(8,128)S(1)}, u32[]{:S(2)}, u32[]{:S(2)}) %collective-permute-start.2) | collective-permute-done | bytes 262176 | tf_op jit(solution)/shard_map/ppermute | solution.py:26
  61.8 0.7 copy-done.1
  62.4 1.3 %broadcast_multiply_fusion = (f32[2,64,16,128]{3,1,2,0:T(8,128)S(1)}, f32[2,16,128,64,1]{2,3,4,1,0:T(8,128)S(1)}) fusion(f32[64,16,128]{2,0,1:T(8,128)S(1)} %copy-done.1, f32[1,64,64]{2,1,0:T(8,128)S(1)} %get-tuple-element.30, f32[1,64,64]{2,1,0:T(8,128)S(1)} %get-tuple-element.31, f32[1,2,64,16,128]{4,2,0,3,1:T(8,128)S(1)} %maximum_bitcast_fusion.1, ...), kind=kOutput, calls=%fused_computation.58 | convolution fusion | flops 403447808 | bytes 4751360 | tf_op jit(solution)/shard_map/tkn,tpnbc->pkbc/dot_general | solution.py:60
  64.5 1.3 %fusion.16 = f32[2,64,16,128]{3,1,0,2:T(8,128)S(1)} fusion(f32[1,64,64]{2,1,0:T(8,128)S(1)} %get-tuple-element.31, f32[1,64,64]{2,1,0:T(8,128)S(1)} %broadcast_multiply_fusion.2, f32[1,2,64,16,128]{4,2,3,1,0:T(8,128)S(1)} %maximum_bitcast_fusion.2, f32[1,2,64,16,128]{4,2,3,1,0:T(8,128)S(1)} %bitcast.155), kind=kOutput, calls=%fused_computation.29 | convolution fusion | flops 403185664 | bytes 3178496 | tf_op jit(solution)/shard_map/tkn,tpnbc->pkbc/dot_general | solution.py:60
  65.8 1.6 %copy.50 = f32[2,64,16,128]{3,2,0,1:T(8,128)} copy(f32[2,64,16,128]{3,1,0,2:T(8,128)S(1)} %fusion.16) | data formatting | bytes 2097152 | tf_op jit(solution)/shard_map/tkn,tpnbc->pkbc/transpose | solution.py:60
  67.4 3.9 %all-to-all-start = ((f32[2,64,16,128]{3,2,0,1:T(8,128)}), f32[2,64,16,128]{3,2,0,1:T(8,128)S(1)}, u32[]{:S(2)}, u32[]{:S(2)}) async-start(f32[2,64,16,128]{3,2,0,1:T(8,128)} %copy.50), calls=%async_computation | async-start | bytes 2097152 | tf_op jit(solution)/shard_map/all_to_all | solution.py:135
  72.5 26.4 %fusion.25 = f32[2,2,2]{1,2,0:T(2,128)S(1)} fusion(f32[2,2,64,16,128]{4,2,3,1,0:T(8,128)S(1)} %pad_maximum_fusion.3, f32[2,64,16,128]{3,1,2,0:T(8,128)S(1)} %get-tuple-element.24), kind=kOutput, calls=%fused_computation.33 | convolution fusion | flops 12582920 | bytes 3145760 | tf_op jit(solution)/shard_map/pn,tqn->tpq/dot_general | solution.py:145
  98.9 12.2 %psum.7 = f32[2,2,2]{1,2,0:T(2,128)S(1)} all-reduce(f32[2,2,2]{1,2,0:T(2,128)S(1)} %fusion.25), channel_id=1, replica_groups=mesh['blk'=8,'space'=4] {'space'}, use_global_device_ids=true, to_apply=%region_0.1 | all-reduce | flops 8 | bytes 64 | tf_op jit(solution)/shard_map/psum | solution.py:158
  112.6 0.6 bitcast_select_fusion.1
  114.1 1.3 %fusion.8 = f32[2,16,128,64,1]{2,3,0,1,4:T(8,128)S(1)} fusion(f32[1,64,64]{2,1,0:T(8,128)S(1)} %get-tuple-element.31, f32[1,64,64]{2,1,0:T(8,128)S(1)} %broadcast_multiply_fusion.2, f32[1,2,16,64,128]{4,3,2,1,0:T(8,128)S(1)} %maximum_bitcast_fusion.3, f32[1,2,16,64,128]{4,3,2,1,0:T(8,128)S(1)} %bitcast.154), kind=kOutput, calls=%fused_computation.21 | convolution fusion | flops 403185664 | bytes 3178496 | tf_op jit(solution)/shard_map/tkn,tpanc->pakc/dot_general | solution.py:67
  115.4 1.0 convolution_multiply_fusion
  116.5 0.6 gather_fusion
  117.1 1.2 bitcast_select_fusion
  (51 shorter events, 10.0 us)
Async XLA Ops:
  0.6 27.3 %collective-permute-start = (bf16[1,8,2,16,4096]{4,3,2,1,0:T(8,128)(2,1)}, bf16[1,8,2,16,4096]{4,3,2,1,0:T(8,128)(2,1)S(1)}, u32[]{:S(2)}, u32[]{:S(2)}) collective-permute-start(bf16[1,8,2,16,4096]{4,3,2,1,0:T(8,128)(2,1)} %param.4), channel_id=1, source_target_pairs={{28,0},{0,4},{4,8},{8,12},{12,16},{16,20},{20,24},{24,28},{29,1},{... | collective-permute-start | bytes 6291464 | tf_op jit(solution)/shard_map/ppermute | solution.py:34
  4.4 2.2 %copy-start = (bf16[1,8,2,16,4096]{4,3,2,1,0:T(8,128)(2,1)S(1)}, bf16[1,8,2,16,4096]{4,3,2,1,0:T(8,128)(2,1)}, u32[]{:S(2)}) copy-start(bf16[1,8,2,16,4096]{4,3,2,1,0:T(8,128)(2,1)} %param.3) | copy-start | bytes 6291460
  34.2 9.1 %collective-permute-start.1 = (f32[2,16,16,128]{3,2,1,0:T(8,128)S(1)}, f32[2,16,16,128]{3,2,1,0:T(8,128)S(1)}, u32[]{:S(2)}, u32[]{:S(2)}) collective-permute-start(f32[2,16,16,128]{3,2,1,0:T(8,128)S(1)} %get-tuple-element.20), channel_id=1, source_target_pairs={{0,1},{1,0},{2,3},{3,2},{4,5},{5,4},{6,7},{7,6},{8,9},{9,8},{10,11... | collective-permute-start | bytes 786440 | tf_op jit(solution)/shard_map/ppermute | solution.py:26
  36.7 24.1 %collective-permute-start.3 = (f32[2,16,16,128]{3,2,1,0:T(8,128)S(1)}, f32[2,16,16,128]{3,2,1,0:T(8,128)S(1)}, u32[]{:S(2)}, u32[]{:S(2)}) collective-permute-start(f32[2,16,16,128]{3,2,1,0:T(8,128)S(1)} %get-tuple-element.18), channel_id=1, source_target_pairs={{0,3},{1,2},{2,1},{3,0},{4,7},{5,6},{6,5},{7,4},{8,11},{9,10},{10,... | collective-permute-start | bytes 786440 | tf_op jit(solution)/shard_map/ppermute | solution.py:26
  39.3 21.5 %collective-permute-start.2 = (f32[2,16,16,128]{3,2,1,0:T(8,128)S(1)}, f32[2,16,16,128]{3,2,1,0:T(8,128)S(1)}, u32[]{:S(2)}, u32[]{:S(2)}) collective-permute-start(f32[2,16,16,128]{3,2,1,0:T(8,128)S(1)} %get-tuple-element.19), channel_id=1, source_target_pairs={{0,2},{1,3},{2,0},{3,1},{4,6},{5,7},{6,4},{7,5},{8,10},{9,11},{10,... | collective-permute-start | bytes 786440 | tf_op jit(solution)/shard_map/ppermute | solution.py:26
  61.4 1.0 copy-start.1
  67.4 45.8 %all-to-all-start = ((f32[2,64,16,128]{3,2,0,1:T(8,128)}), f32[2,64,16,128]{3,2,0,1:T(8,128)S(1)}, u32[]{:S(2)}, u32[]{:S(2)}) async-start(f32[2,64,16,128]{3,2,0,1:T(8,128)} %copy.50), calls=%async_computation | async-start | bytes 2097152 | tf_op jit(solution)/shard_map/all_to_all | solution.py:135
